TPU v7x, 32 devices: a whole 2x2x4 slice. The times are simulated.
32 devices in a mesh: dp: 8 (over z, y), grp: 4 (over x, core).
Axes of the slice: x: 2, y: 2, z: 4, core: 2. Of those that a mesh axis runs over, the one named last changes fastest.
Arguments:
- activations: bfloat16 [32, 512, 768], P('dp', None, 'grp'), may hold values from -6 to 6, as said below
- cotangent: bfloat16 [32, 512, 768], P('dp', None, 'grp'), may hold values from -6 to 6
- lengths: int32 [32], P('dp'), may hold values from 64 to 512
- triple_weight: bfloat16 [2, 4, 192, 576], P(None, 'grp'), may hold values from -0.25980762 to 0.25980762, as said below
- triple_bias: float32 [2, 2, 768], P(None, None, 'grp'), may hold values from -1.8 to 1.8, as said below
- output_weight: bfloat16 [2, 768, 768], replicated, may hold values from -1.75 to 1.75
- output_bias: float32 [2, 768], replicated, may hold values from -1.75 to 1.75
- first_gain: float32 [2, 768], replicated, may hold values from 0.25 to 1.75
- first_shift: float32 [2, 768], replicated, may hold values from -1.75 to 1.75
- widen_weight: bfloat16 [2, 4, 192, 768], P(None, 'grp'), may hold values from -0.4375 to 0.4375
- widen_bias: float32 [2, 3072], P(None, 'grp'), may hold values from -1.75 to 1.75
- shrink_weight: bfloat16 [2, 4, 768, 192], P(None, 'grp'), may hold values from -0.21875 to 0.21875
- narrow_bias: float32 [2, 768], P(None, 'grp'), may hold values from -1.75 to 1.75
- second_gain: float32 [2, 768], P(None, 'grp'), may hold values from 0.25 to 1.75
- second_shift: float32 [2, 768], P(None, 'grp'), may hold values from -1.75 to 1.75
Outputs:
- layer_output: bfloat16 [32, 512, 768], P('dp', None, 'grp')
- input_gradient: float32 [32, 512, 768], P('dp', None, 'grp')
- triple_weight_gradient: float32 [2, 4, 192, 576], P(None, 'grp')
- triple_bias_gradient: float32 [2, 2, 768], P(None, None, 'grp')
- output_weight_gradient: float32 [2, 768, 768], replicated
- output_bias_gradient: float32 [2, 768], replicated
- first_gain_gradient: float32 [2, 768], replicated
- first_shift_gradient: float32 [2, 768], replicated
- widen_weight_gradient: float32 [2, 4, 192, 768], P(None, 'grp')
- widen_bias_gradient: float32 [2, 3072], P(None, 'grp')
- narrow_weight_gradient: float32 [2, 4, 768, 192], P(None, 'grp')
- narrow_bias_gradient: float32 [2, 768], P(None, 'grp')
- second_norm_gain_gradient: float32 [2, 768], P(None, 'grp')
- second_shift_gradient: float32 [2, 768], P(None, 'grp')
Inputs may be any that keep to these rules, and one draw needn't show every extreme that they name: `activations`: independent entries of order one. `triple_weight`: independent entries with deviation about 192 ** -0.5. `triple_bias`: independent entries with deviation about 0.3.
All inputs are finite; a program needn't handle non-finite values.
Results may differ from a plain program's by a relative error of at most 0.015.
Values may be sent and summed in bfloat16 or wider, within the bound.
A program may use at most 192 MiB of HBM per device.

v0:
```python
import math

import jax
import jax.numpy as jnp
from jax import lax
from jax.sharding import PartitionSpec as P

HEAD = 64


EPSILON = 1e-05
MASKED = -1e30


def contract_rows(left, right):
    return lax.dot_general(
        left, right, (((0,), (0,)), ((), ())), preferred_element_type=jnp.float32
    )


def contract_cols(left, weight):
    return lax.dot_general(
        left, weight, (((1,), (1,)), ((), ())), preferred_element_type=jnp.float32
    )


def split_heads(block):
    return block.reshape(block.shape[0], block.shape[1] // HEAD, HEAD)


def score_block(queries, keys, length):
    scores = jnp.einsum(
        "qhd,khd->hqk", split_heads(queries), split_heads(keys), preferred_element_type=jnp.float32
    ) * HEAD ** (-0.5)
    visible = jnp.arange(keys.shape[0]) < length
    return jnp.where(visible[None, None, :], scores, MASKED)


def attend_forward(queries, keys, values, lengths):

    def single(inputs):
        query_one, key_one, value_one, length = inputs
        scores = score_block(query_one, key_one, length)
        highest = jnp.max(scores, axis=-1, keepdims=True)
        expon = jnp.exp(scores - highest)
        totals = jnp.sum(expon, axis=-1, keepdims=True)
        weights = (expon / totals).astype(jnp.bfloat16)
        mixed = jnp.einsum(
            "hqk,khd->qhd", weights, split_heads(value_one), preferred_element_type=jnp.float32
        )
        return (mixed.reshape(query_one.shape).astype(jnp.bfloat16), highest, totals)

    return lax.map(single, (queries, keys, values, lengths))


def attend_backward(queries, keys, values, outgrad, highest, totals, lengths):

    def single(inputs):
        query_one, key_one, value_one, grad_one, top, total, length = inputs
        scores = score_block(query_one, key_one, length)
        probs = jnp.exp(scores - top) / total
        weights = probs.astype(jnp.bfloat16)
        grad_heads = split_heads(grad_one)
        grad_probs = jnp.einsum(
            "qhd,khd->hqk", grad_heads, split_heads(value_one), preferred_element_type=jnp.float32
        )
        inner = jnp.sum(probs * grad_probs, axis=-1, keepdims=True)
        grad_scores = (probs * (grad_probs - inner)).astype(jnp.bfloat16)
        factor = HEAD ** (-0.5)
        query_grad = (
            jnp.einsum(
                "hqk,khd->qhd",
                grad_scores,
                split_heads(key_one),
                preferred_element_type=jnp.float32,
            )
            * factor
        )
        key_grad = (
            jnp.einsum(
                "hqk,qhd->khd",
                grad_scores,
                split_heads(query_one),
                preferred_element_type=jnp.float32,
            )
            * factor
        )
        value_grad = jnp.einsum(
            "hqk,qhd->khd", weights, grad_heads, preferred_element_type=jnp.float32
        )
        shape = query_one.shape
        return (
            query_grad.reshape(shape).astype(jnp.bfloat16),
            key_grad.reshape(shape).astype(jnp.bfloat16),
            value_grad.reshape(shape).astype(jnp.bfloat16),
        )

    return lax.map(single, (queries, keys, values, outgrad, highest, totals, lengths))


def gelu_slope(values):
    return 0.5 * (1.0 + lax.erf(values / math.sqrt(2.0))) + values * jnp.exp(
        -0.5 * values * values
    ) / math.sqrt(2.0 * math.pi)


def layer_forward(inputs, lengths, params, layer_params):
    (
        triple_weight,
        triple_bias,
        output_weight,
        output_bias,
        first_gain,
        first_shift,
        widen_weight,
        widen_bias,
        shrink_weight,
        narrow_bias,
        second_gain,
        second_shift,
    ) = params
    group_width = inputs.shape[-1]
    rows = inputs.reshape(-1, group_width)
    projected = jnp.dot(rows, triple_weight[layer_params, 0], preferred_element_type=jnp.float32)
    queries = (
        (projected[:, :group_width] + triple_bias[layer_params, 0])
        .astype(jnp.bfloat16)
        .reshape(inputs.shape)
    )
    keys = projected[:, group_width : 2 * group_width].astype(jnp.bfloat16).reshape(inputs.shape)
    values = (
        (projected[:, 2 * group_width :] + triple_bias[layer_params, 1])
        .astype(jnp.bfloat16)
        .reshape(inputs.shape)
    )
    queries, keys, values, residual = (
        lax.all_to_all(queries, "grp", split_axis=0, concat_axis=2, tiled=True),
        lax.all_to_all(keys, "grp", split_axis=0, concat_axis=2, tiled=True),
        lax.all_to_all(values, "grp", split_axis=0, concat_axis=2, tiled=True),
        lax.all_to_all(inputs, "grp", split_axis=0, concat_axis=2, tiled=True),
    )
    local = queries.shape[0]
    mine = lax.dynamic_slice_in_dim(lengths, lax.axis_index("grp") * local, local)
    attended, highest, totals = attend_forward(queries, keys, values, mine)
    width = attended.shape[-1]
    flat = attended.reshape(-1, width)
    before = (
        residual.reshape(-1, width).astype(jnp.float32)
        + jnp.dot(flat, output_weight[layer_params], preferred_element_type=jnp.float32)
        + output_bias[layer_params]
    )
    center = before - jnp.mean(before, axis=-1, keepdims=True)
    first_inverse = lax.rsqrt(jnp.mean(center * center, axis=-1, keepdims=True) + EPSILON)
    first_normed = center * first_inverse
    hidden = (
        (first_normed * first_gain[layer_params] + first_shift[layer_params])
        .astype(jnp.bfloat16)
        .reshape(attended.shape)
    )
    hidden_group = lax.all_to_all(hidden, "grp", split_axis=2, concat_axis=0, tiled=True)
    group_rows = hidden_group.reshape(-1, group_width)
    widened = (
        jnp.dot(group_rows, widen_weight[layer_params, 0], preferred_element_type=jnp.float32)
        + widen_bias[layer_params]
    )
    gelu_output = jax.nn.gelu(widened, approximate=False).astype(jnp.bfloat16)
    after = (
        group_rows.astype(jnp.float32)
        + jnp.dot(gelu_output, shrink_weight[layer_params, 0], preferred_element_type=jnp.float32)
        + narrow_bias[layer_params]
    )
    row_sum = jnp.sum(after, axis=-1)
    row_square = jnp.sum(after * after, axis=-1)
    total_sum, total_square = lax.psum((row_sum, row_square), "grp")
    average = (total_sum / width)[:, None]
    variance = (total_square / width)[:, None] - average * average
    second_inverse = lax.rsqrt(variance + EPSILON)
    second_normed = (after - average) * second_inverse
    output = (second_normed * second_gain[layer_params] + second_shift[layer_params]).reshape(
        inputs.shape
    )
    kept = (
        inputs,
        queries,
        keys,
        values,
        mine,
        highest,
        totals,
        attended,
        first_normed,
        first_inverse,
        group_rows,
        widened,
        gelu_output,
        second_normed,
        second_inverse,
    )
    return (output, kept)


def layer_backward(outgrad, params, layer_params, kept):
    (
        triple_weight,
        triple_bias,
        output_weight,
        output_bias,
        first_gain,
        first_shift,
        widen_weight,
        widen_bias,
        shrink_weight,
        narrow_bias,
        second_gain,
        second_shift,
    ) = params
    (
        inputs,
        queries,
        keys,
        values,
        mine,
        highest,
        totals,
        attended,
        first_normed,
        first_inverse,
        group_rows,
        widened,
        gelu_output,
        second_normed,
        second_inverse,
    ) = kept
    group_width = inputs.shape[-1]
    width = attended.shape[-1]
    grad_rows = outgrad.reshape(-1, group_width)
    scaled = grad_rows * second_gain[layer_params]
    part_sum = jnp.sum(scaled, axis=-1)
    part_cross = jnp.sum(scaled * second_normed, axis=-1)
    total_sum, total_cross = lax.psum((part_sum, part_cross), "grp")
    grad_after = second_inverse * (
        scaled - (total_sum / width)[:, None] - second_normed * (total_cross / width)[:, None]
    )
    second_gain_grad = jnp.sum(grad_rows * second_normed, axis=0)
    second_shift_grad = jnp.sum(grad_rows, axis=0)
    narrow_rounded = grad_after.astype(jnp.bfloat16)
    narrow_weight_grad = contract_rows(gelu_output, narrow_rounded)
    narrow_bias_grad = jnp.sum(narrow_rounded.astype(jnp.float32), axis=0)
    gelu_output_gradient = contract_cols(narrow_rounded, shrink_weight[layer_params, 0])
    widened_grad = (gelu_output_gradient * gelu_slope(widened)).astype(jnp.bfloat16)
    widen_weight_grad = contract_rows(group_rows, widened_grad)
    widen_bias_grad = jnp.sum(widened_grad.astype(jnp.float32), axis=0)
    hidden_grad = (grad_after + contract_cols(widened_grad, widen_weight[layer_params, 0])).astype(
        jnp.bfloat16
    )
    hidden_seq = lax.all_to_all(
        hidden_grad.reshape(inputs.shape), "grp", split_axis=0, concat_axis=2, tiled=True
    )
    seq_rows = hidden_seq.reshape(-1, width).astype(jnp.float32)
    first_gain_grad = jnp.sum(seq_rows * first_normed, axis=0)
    first_shift_grad = jnp.sum(seq_rows, axis=0)
    scaled_first = seq_rows * first_gain[layer_params]
    grad_before = first_inverse * (
        scaled_first
        - jnp.mean(scaled_first, axis=-1, keepdims=True)
        - first_normed * jnp.mean(scaled_first * first_normed, axis=-1, keepdims=True)
    )
    before_rounded = grad_before.astype(jnp.bfloat16)
    flat = attended.reshape(-1, width)
    output_weight_grad = contract_rows(flat, before_rounded)
    output_bias_grad = jnp.sum(before_rounded.astype(jnp.float32), axis=0)
    attended_grad = (
        contract_cols(before_rounded, output_weight[layer_params])
        .astype(jnp.bfloat16)
        .reshape(attended.shape)
    )
    residual_grad = before_rounded.reshape(attended.shape)
    query_seq, key_seq, value_seq = attend_backward(
        queries, keys, values, attended_grad, highest, totals, mine
    )
    query_grad, key_grad, value_grad, input_part = (
        lax.all_to_all(query_seq, "grp", split_axis=2, concat_axis=0, tiled=True),
        lax.all_to_all(key_seq, "grp", split_axis=2, concat_axis=0, tiled=True),
        lax.all_to_all(value_seq, "grp", split_axis=2, concat_axis=0, tiled=True),
        lax.all_to_all(residual_grad, "grp", split_axis=2, concat_axis=0, tiled=True),
    )
    triple_grad = jnp.concatenate(
        [
            query_grad.reshape(-1, group_width),
            key_grad.reshape(-1, group_width),
            value_grad.reshape(-1, group_width),
        ],
        axis=-1,
    )
    triple_weight_grad = contract_rows(inputs.reshape(-1, group_width), triple_grad)
    triple_bias_grad = jnp.stack(
        [
            jnp.sum(query_grad.reshape(-1, group_width).astype(jnp.float32), axis=0),
            jnp.sum(value_grad.reshape(-1, group_width).astype(jnp.float32), axis=0),
        ]
    )
    input_grad = contract_cols(triple_grad, triple_weight[layer_params, 0]) + input_part.reshape(
        -1, group_width
    ).astype(jnp.float32)
    grads = (
        triple_weight_grad[None],
        triple_bias_grad,
        output_weight_grad,
        output_bias_grad,
        first_gain_grad,
        first_shift_grad,
        widen_weight_grad[None],
        widen_bias_grad,
        narrow_weight_grad[None],
        narrow_bias_grad,
        second_gain_grad,
        second_shift_grad,
    )
    return (input_grad.reshape(inputs.shape), grads)


def shards(
    activations,
    cotangent,
    lengths,
    triple_weight,
    triple_bias,
    output_weight,
    output_bias,
    first_gain,
    first_shift,
    widen_weight,
    widen_bias,
    shrink_weight,
    narrow_bias,
    second_gain,
    second_shift,
):
    params = (
        triple_weight,
        triple_bias,
        output_weight,
        output_bias,
        first_gain,
        first_shift,
        widen_weight,
        widen_bias,
        shrink_weight,
        narrow_bias,
        second_gain,
        second_shift,
    )
    depth = triple_weight.shape[0]
    current = activations
    stored = []
    kept_list = []
    final = None
    for layer_params in range(depth):
        stored.append(current)
        result, kept = layer_forward(current, lengths, params, layer_params)
        kept_list.append(kept)
        final = result
        current = result.astype(jnp.bfloat16)
    outgrad = cotangent.astype(jnp.float32)
    collected = [None] * depth
    for layer_params in reversed(range(depth)):
        replayed, kept = layer_forward(stored[layer_params], lengths, params, layer_params)
        outgrad, layer_param_gradients = layer_backward(outgrad, params, layer_params, kept)
        collected[layer_params] = layer_param_gradients
    stacked = [
        jnp.stack([collected[layer_params][member] for layer_params in range(depth)])
        for member in range(12)
    ]
    group_totals = lax.psum(
        (
            stacked[0],
            stacked[1],
            stacked[6],
            stacked[7],
            stacked[8],
            stacked[9],
            stacked[10],
            stacked[11],
        ),
        "dp",
    )
    shared_totals = lax.psum((stacked[2], stacked[3], stacked[4], stacked[5]), ("dp", "grp"))
    return (
        final.astype(jnp.bfloat16),
        outgrad,
        group_totals[0],
        group_totals[1],
        shared_totals[0],
        shared_totals[1],
        shared_totals[2],
        shared_totals[3],
        group_totals[2],
        group_totals[3],
        group_totals[4],
        group_totals[5],
        group_totals[6],
        group_totals[7],
    )


def solution(mesh):
    in_specs = (
        P("dp", None, "grp"),
        P("dp", None, "grp"),
        P("dp"),
        P(None, "grp", None, None),
        P(None, None, "grp"),
        P(),
        P(),
        P(),
        P(),
        P(None, "grp", None, None),
        P(None, "grp"),
        P(None, "grp", None, None),
        P(None, "grp"),
        P(None, "grp"),
        P(None, "grp"),
    )
    out_specs = (
        P("dp", None, "grp"),
        P("dp", None, "grp"),
        P(None, "grp", None, None),
        P(None, None, "grp"),
        P(),
        P(),
        P(),
        P(),
        P(None, "grp", None, None),
        P(None, "grp"),
        P(None, "grp", None, None),
        P(None, "grp"),
        P(None, "grp"),
        P(None, "grp"),
    )
    return jax.shard_map(shards, mesh=mesh, in_specs=in_specs, out_specs=out_specs, check_vma=False)
```

profile of v0, /device:TPU:0, one launch (start us, length us, event | category | flops | bytes accessed | tf_op | source)
XLA Modules:
  0.0 857.7 jit_solution(8457950099970390052)
XLA Ops:
  7.2 4.4 all-to-all-start
  17.0 6.2 all-to-all-done
  31.4 6.9 all-to-all-done.3
  38.3 4.2 all-to-all-start.2
  45.1 9.1 %all-to-all-done.2 = bf16[4,512,192]{1,2,0:T(8,128)(2,1)} async-done(((bf16[4,512,192]{1,2,0:T(8,128)(2,1)}), bf16[4,512,192]{1,2,0:T(8,128)(2,1)}, u32[]{:S(2)}, u32[]{:S(2)}) %all-to-all-start.2) | async-done | bytes 786464 | tf_op jit(solution)/shard_map/all_to_all | solution.py:137
  57.7 10.6 %fusion.129 = (f32[12,512]{1,0:T(8,128)S(1)}, f32[12,512,512]{1,2,0:T(8,128)}) fusion(pred[512]{0:T(512)(128)(4,1)S(1)} %iota_compare_fusion, bf16[512,12,64]{0,2,1:T(8,128)(2,1)} %bitcast.12, bf16[512,12,64]{0,2,1:T(8,128)(2,1)S(1)} %bitcast.431), kind=kOutput, calls=%fused_computation.281 | convolution fusion | flops 415236608 | bytes 14180864 | tf_op jit(solution)/shard_map/while/body/eval_jaxpr/sub | solution.py:45
  69.4 6.1 fusion.61
  80.1 5.4 reduce.28
  91.6 10.4 %all-to-all-done.4 = bf16[4,2,49152]{2,1,0:T(2,128)(2,1)S(1)} async-done(((bf16[4,2,49152]{2,1,0:T(2,128)(2,1)}), bf16[4,2,49152]{2,1,0:T(2,128)(2,1)S(1)}, u32[]{:S(2)}, u32[]{:S(2)}) %all-to-all-start.4) | async-done | bytes 786464 | tf_op jit(solution)/shard_map/all_to_all | solution.py:160
  103.8 15.9 %fusion.6 = (bf16[2048,768]{1,0:T(8,128)(2,1)S(1)}, f32[2048,768]{1,0:T(8,128)}) fusion(f32[768]{0:T(1024)S(1)} %get-tuple-element.241, bf16[2048,192]{0,1:T(8,128)(2,1)S(1)} %bitcast.493, bf16[2,1,192,768]{3,2,1,0:T(8,128)(2,1)S(1)} %copy-done.66), kind=kOutput, calls=%fused_computation.18 | convolution fusion | flops 707788800 | bytes 10522624 | tf_op jit(solution)/shard_map/dot_general | solution.py:163
  121.4 10.1 %all-reduce.6 = (f32[2048]{0:T(1024)S(1)}, f32[2048]{0:T(1024)S(1)}) all-reduce(f32[2048]{0:T(1024)S(1)} %get-tuple-element.233, f32[2048]{0:T(1024)S(1)} %get-tuple-element.232), channel_id=1, replica_groups=mesh['dp'=8,'grp'=4] {'grp'}, use_global_device_ids=true, to_apply=%region_7.8 | all-reduce | flops 4096 | bytes 32768 | tf_op jit(solution)/shard_map/psum | solution.py:174
  142.1 6.6 all-to-all-done.5
  148.7 3.9 all-to-all-start.8
  155.7 8.5 all-to-all-done.8
  164.2 4.2 all-to-all-start.7
  171.2 8.9 %all-to-all-done.7 = bf16[4,512,192]{1,2,0:T(8,128)(2,1)} async-done(((bf16[4,512,192]{1,2,0:T(8,128)(2,1)}), bf16[4,512,192]{1,2,0:T(8,128)(2,1)}, u32[]{:S(2)}, u32[]{:S(2)}) %all-to-all-start.7) | async-done | bytes 786464 | tf_op jit(solution)/shard_map/all_to_all | solution.py:137
  183.7 10.5 %fusion.131 = (f32[12,512]{1,0:T(8,128)S(1)}, f32[12,512,512]{1,2,0:T(8,128)}) fusion(pred[512]{0:T(512)(128)(4,1)S(1)} %iota_compare_fusion, bf16[512,12,64]{0,2,1:T(8,128)(2,1)} %bitcast.37, bf16[512,12,64]{0,2,1:T(8,128)(2,1)S(1)} %bitcast.433), kind=kOutput, calls=%fused_computation.283 | convolution fusion | flops 415236608 | bytes 14180864 | tf_op jit(solution)/shard_map/while/body/eval_jaxpr/sub | solution.py:45
  195.3 6.1 fusion.67
  207.6 6.3 reduce.29
  216.3 4.2 all-to-all-start.9
  221.9 10.4 %all-to-all-done.9 = bf16[4,2,49152]{2,1,0:T(2,128)(2,1)} async-done(((bf16[4,2,49152]{2,1,0:T(2,128)(2,1)}), bf16[4,2,49152]{2,1,0:T(2,128)(2,1)}, u32[]{:S(2)}, u32[]{:S(2)}) %all-to-all-start.9) | async-done | bytes 786464 | tf_op jit(solution)/shard_map/all_to_all | solution.py:160
  232.3 3.7 reshape.510
  238.5 15.8 %fusion.9 = (bf16[2048,768]{1,0:T(8,128)(2,1)S(1)}, f32[2048,768]{1,0:T(8,128)}) fusion(f32[768]{0:T(1024)S(1)} %get-tuple-element.240, bf16[2048,192]{0,1:T(8,128)(2,1)S(1)} %bitcast.497, bf16[2,1,192,768]{3,2,1,0:T(8,128)(2,1)S(1)} %copy-done.67), kind=kOutput, calls=%fused_computation.21 | convolution fusion | flops 707788800 | bytes 10522624 | tf_op jit(solution)/shard_map/dot_general | solution.py:163
  256.7 10.3 %all-reduce.5 = (f32[2048]{0:T(1024)S(1)}, f32[2048]{0:T(1024)S(1)}) all-reduce(f32[2048]{0:T(1024)S(1)} %get-tuple-element.231, f32[2048]{0:T(1024)S(1)} %get-tuple-element.230), channel_id=1, replica_groups=mesh['dp'=8,'grp'=4] {'grp'}, use_global_device_ids=true, to_apply=%region_15.16 | all-reduce | flops 4096 | bytes 32768 | tf_op jit(solution)/shard_map/psum | solution.py:174
  269.4 10.3 %all-reduce.4 = (f32[2048]{0:T(1024)S(1)}, f32[2048]{0:T(1024)S(1)}) all-reduce(f32[2048]{0:T(1024)S(1)} %get-tuple-element.223, f32[2048]{0:T(1024)S(1)} %bitcast.523), channel_id=1, replica_groups=mesh['dp'=8,'grp'=4] {'grp'}, use_global_device_ids=true, to_apply=%region_19.20 | all-reduce | flops 4096 | bytes 32768 | tf_op jit(solution)/shard_map/psum | solution.py:240
  279.8 4.1 convert_reduce_fusion.3
  283.9 6.3 convert_reduce_fusion
  292.9 4.2 all-to-all-start.10
  297.1 11.6 %all-to-all-done.10 = bf16[4,512,192]{1,2,0:T(8,128)(2,1)} async-done(((bf16[4,512,192]{1,2,0:T(8,128)(2,1)}), bf16[4,512,192]{1,2,0:T(8,128)(2,1)}, u32[]{:S(2)}, u32[]{:S(2)}) %all-to-all-start.10) | async-done | bytes 786464 | tf_op jit(solution)/shard_map/all_to_all | solution.py:256
  322.4 6.9 fusion.70
  330.5 6.3 reduce.33
  339.2 3.9 all-to-all-start.13
  343.1 11.6 %multiply_reduce_fusion.1 = (f32[12,512]{1,0:T(8,128)S(1)}, f32[12,512,512]{1,2,0:T(8,128)}) fusion(f32[12,512,512]{1,2,0:T(8,128)} %get-tuple-element.302, f32[12,512]{1,0:T(8,128)S(1)} %get-tuple-element.301, bf16[512,12,64]{0,2,1:T(8,128)(2,1)} %bitcast.513, bf16[512,12,64]{0,2,1:T(8,128)(2,1)} %bitcast.510), kind=kOutput, calls=%fused_computation.5 | convolution fusion | flops 412084224 | bytes 26787840 | tf_op jit(solution)/shard_map/while/body/eval_jaxpr/qhd,khd->hqk/dot_general | solution.py:64
  357.6 6.4 reduce.30
  365.3 4.4 all-to-all-start.14
  369.7 9.6 %multiply_convert_fusion.1 = bf16[12,512,512]{1,2,0:T(8,128)(2,1)S(1)} fusion(f32[12,512,512]{1,2,0:T(8,128)} %get-tuple-element.309, f32[12,512]{1,0:T(8,128)S(1)} %get-tuple-element.308, f32[12,512,512]{1,2,0:T(8,128)} %get-tuple-element.302, f32[12,512]{1,0:T(8,128)S(1)} %get-tuple-element.301), kind=kLoop, calls=%fused_computation.4 | loop fusion | flops 12582912 | bytes 31506432 | tf_op jit(solution)/shard_map/while/body/eval_jaxpr/convert_element_type | solution.py:68
  379.4 3.7 multiply_convert_fusion.5
  385.4 6.5 reduce.32
  393.3 4.4 all-to-all-start.12
  397.8 3.9 multiply_convert_fusion.6
  404.1 6.4 reduce.31
  411.8 4.4 all-to-all-start.11
  441.0 11.9 %all-reduce.3 = (f32[2048]{0:T(1024)S(1)}, f32[2048]{0:T(1024)S(1)}) all-reduce(f32[2048]{0:T(1024)S(1)} %get-tuple-element.221, f32[2048]{0:T(1024)S(1)} %get-tuple-element.228), channel_id=1, replica_groups=mesh['dp'=8,'grp'=4] {'grp'}, use_global_device_ids=true, to_apply=%region_26.27 | all-reduce | flops 4096 | bytes 32768 | tf_op jit(solution)/shard_map/psum | solution.py:240
  454.9 6.3 convert_reduce_fusion.1
  463.9 4.8 all-to-all-start.15
  476.6 3.8 all-to-all-done.15
  489.5 6.7 fusion.64
  496.2 8.6 %multiply_reduce_fusion = (f32[12,512]{1,0:T(8,128)S(1)}, f32[12,512,512]{1,2,0:T(8,128)}) fusion(f32[12,512,512]{1,2,0:T(8,128)} %get-tuple-element.295, f32[12,512]{1,0:T(8,128)S(1)} %copy-done.81, bf16[512,12,64]{0,2,1:T(8,128)(2,1)S(1)} %bitcast.515, bf16[512,12,64]{0,2,1:T(8,128)(2,1)S(1)} %bitcast.508), kind=kOutput, calls=%fused_computation.3 | convolution fusion | flops 412084224 | bytes 26787840 | tf_op jit(solution)/shard_map/while/body/eval_jaxpr/qhd,khd->hqk/dot_general | solution.py:64
  506.0 5.4 reduce.37
  512.8 4.4 all-to-all-start.18
  517.2 9.6 %multiply_convert_fusion = bf16[12,512,512]{1,2,0:T(8,128)(2,1)S(1)} fusion(f32[12,512,512]{1,2,0:T(8,128)} %get-tuple-element.312, f32[12,512]{1,0:T(8,128)S(1)} %get-tuple-element.311, f32[12,512,512]{1,2,0:T(8,128)} %get-tuple-element.295, f32[12,512]{1,0:T(8,128)S(1)} %copy-done.81), kind=kLoop, calls=%fused_computation.2 | loop fusion | flops 12582912 | bytes 31506432 | tf_op jit(solution)/shard_map/while/body/eval_jaxpr/convert_element_type | solution.py:68
  526.9 3.7 multiply_convert_fusion.2
  531.8 5.4 reduce.36
  542.1 4.2 all-to-all-start.17
  546.8 4.2 pad_maximum_fusion
  552.1 3.9 multiply_convert_fusion.3
  558.3 7.5 reduce.35
  568.2 4.2 all-to-all-start.16
  601.5 6.3 reduce.34
  610.2 4.2 all-to-all-start.19
  614.6 47.3 %all-reduce = (f32[2,768]{1,0:T(2,128)}, f32[2,768]{1,0:T(2,128)}, f32[2,768]{1,0:T(2,128)}) all-reduce(f32[2,768]{1,0:T(2,128)S(1)} %pad_maximum_fusion.4, f32[2,768]{1,0:T(2,128)S(1)} %pad_maximum_fusion.5, f32[2,768]{1,0:T(2,128)S(1)} %pad_maximum_fusion.6), channel_id=1, replica_groups=mesh['dp'=8,'grp'=4] {'dp','grp'}, use_global_device_ids=true, to_apply=%region_39.40 | all-reduce | flops 4608 | bytes 36864 | tf_op jit(solution)/shard_map/psum | solution.py:387
  669.0 37.9 %all-reduce.1 = (f32[2,2,192]{2,1,0:T(2,128)}, f32[2,768]{1,0:T(2,128)}, f32[2,192]{1,0:T(2,128)}, f32[2,192]{1,0:T(2,128)}, f32[2,192]{1,0:T(2,128)}) all-reduce(f32[2,2,192]{2,1,0:T(2,128)S(1)} %pad_maximum_fusion.8, f32[2,768]{1,0:T(2,128)S(1)} %pad_maximum_fusion.7, ...), channel_id=1, replica_groups=mesh['dp'=8,'grp'=4] {'dp'}, use_global_device_ids=true, to_apply=%region_35.36 | all-reduce | flops 3456 | bytes 27648 | tf_op jit(solution)/shard_map/psum | solution.py:374
  706.8 134.0 %all-reduce.12.cloned.1.call-done = (f32[2,1,192,576]{3,2,1,0:T(8,128)}, f32[2,1,192,768]{3,2,1,0:T(8,128)}, f32[2,1,768,192]{2,3,1,0:T(8,128)}) async-done(((f32[2,1,192,576]{3,2,1,0:T(8,128)}, f32[2,1,192,768]{3,2,1,0:T(8,128)}, f32[2,1,768,192]{2,3,1,0:T(8,128)}), (f32[2,1,192,576]{3,2,1,0:T(8,128)}, f32[2,1,192,768]{3,2,1,0:T(8,128)}, f32[2,1,768,192]{2,3,1,0:T(8,128)})) %all-reduce.12.cloned.1.call-update) | async-done | bytes 3244048 | tf_op jit(solution)/shard_map/psum | solution.py:374
  843.0 4.9 copy.272
  (426 shorter events, 208.4 us)
Async XLA Ops:
  7.2 16.0 %all-to-all-start = ((bf16[4,512,192]{1,2,0:T(8,128)(2,1)}), bf16[4,512,192]{1,2,0:T(8,128)(2,1)S(1)}, u32[]{:S(2)}, u32[]{:S(2)}) async-start(bf16[4,512,192]{1,2,0:T(8,128)(2,1)} %param.15), calls=%async_computation | async-start | bytes 1572864 | tf_op jit(solution)/shard_map/all_to_all | solution.py:140
  15.9 10.8 %copy-start.96 = (f32[2,2,192]{2,1,0:T(2,128)S(1)}, f32[2,2,192]{2,1,0:T(2,128)}, u32[]{:S(2)}) copy-start(f32[2,2,192]{2,1,0:T(2,128)} %param.19) | copy-start | bytes 9220
  23.2 15.1 %all-to-all-start.3 = ((bf16[4,512,192]{1,2,0:T(8,128)(2,1)}), bf16[4,512,192]{1,2,0:T(8,128)(2,1)S(1)}, u32[]{:S(2)}, u32[]{:S(2)}) async-start(bf16[4,512,192]{1,2,0:T(8,128)(2,1)} %bitcast.407), calls=%async_computation.3 | async-start | bytes 1572864 | tf_op jit(solution)/shard_map/all_to_all | solution.py:138
  28.9 14.3 %copy-start.87 = (f32[2,768]{1,0:T(2,128)S(1)}, f32[2,768]{1,0:T(2,128)}, u32[]{:S(2)}) copy-start(f32[2,768]{1,0:T(2,128)} %param.21) | copy-start | bytes 18436
  28.9 14.3 %copy-start.88 = (f32[2,768]{1,0:T(2,128)S(1)}, f32[2,768]{1,0:T(2,128)}, u32[]{:S(2)}) copy-start(f32[2,768]{1,0:T(2,128)} %param.23) | copy-start | bytes 18436
  28.9 14.3 %copy-start.89 = (f32[2,768]{1,0:T(2,128)S(1)}, f32[2,768]{1,0:T(2,128)}, u32[]{:S(2)}) copy-start(f32[2,768]{1,0:T(2,128)} %param.22) | copy-start | bytes 18436
  38.3 19.4 %copy-start.32 = (bf16[4,512,192]{1,2,0:T(8,128)(2,1)}, bf16[4,512,192]{1,2,0:T(8,128)(2,1)S(1)}, u32[]{:S(2)}) copy-start(bf16[4,512,192]{1,2,0:T(8,128)(2,1)S(1)} %all-to-all-done.3) | copy-start | bytes 2359300
  38.3 15.9 %all-to-all-start.2 = ((bf16[4,512,192]{1,2,0:T(8,128)(2,1)}), bf16[4,512,192]{1,2,0:T(8,128)(2,1)}, u32[]{:S(2)}, u32[]{:S(2)}) async-start(bf16[4,512,192]{1,2,0:T(8,128)(2,1)} %bitcast.408), calls=%async_computation.2 | async-start | bytes 1572864 | tf_op jit(solution)/shard_map/all_to_all | solution.py:137
  43.3 33.6 %copy-start.74 = (f32[768]{0:T(1024)}, f32[768]{0:T(1024)S(1)}, u32[]{:S(2)}) copy-start(f32[768]{0:T(1024)S(1)} %get-tuple-element.317) | copy-start | bytes 9220
  54.2 15.1 %all-to-all-start.1 = ((bf16[4,512,192]{1,2,0:T(8,128)(2,1)}), bf16[4,512,192]{1,2,0:T(8,128)(2,1)S(1)}, u32[]{:S(2)}, u32[]{:S(2)}) async-start(bf16[4,512,192]{1,2,0:T(8,128)(2,1)} %bitcast.409), calls=%async_computation.1 | async-start | bytes 1572864 | tf_op jit(solution)/shard_map/all_to_all | solution.py:139
  68.3 7.1 copy-start.80
  76.8 8.7 %copy-start.78 = (f32[512]{0:T(512)}, f32[512]{0:T(512)S(1)}, u32[]{:S(2)}) copy-start(f32[512]{0:T(512)S(1)} %add_rsqrt_fusion.3) | copy-start | bytes 6148
  79.5 10.9 %copy-start.99 = (f32[2,192]{1,0:T(2,128)S(1)}, f32[2,192]{1,0:T(2,128)}, u32[]{:S(2)}) copy-start(f32[2,192]{1,0:T(2,128)} %param.27) | copy-start | bytes 4612
  79.5 11.5 %copy-start.90 = (f32[2,768]{1,0:T(2,128)S(1)}, f32[2,768]{1,0:T(2,128)}, u32[]{:S(2)}) copy-start(f32[2,768]{1,0:T(2,128)} %param.25) | copy-start | bytes 18436
  79.5 11.5 %copy-start.100 = (f32[2,192]{1,0:T(2,128)S(1)}, f32[2,192]{1,0:T(2,128)}, u32[]{:S(2)}) copy-start(f32[2,192]{1,0:T(2,128)} %param.28) | copy-start | bytes 4612
  79.5 11.5 %copy-start.101 = (f32[2,192]{1,0:T(2,128)S(1)}, f32[2,192]{1,0:T(2,128)}, u32[]{:S(2)}) copy-start(f32[2,192]{1,0:T(2,128)} %param.29) | copy-start | bytes 4612
  86.9 15.1 %all-to-all-start.4 = ((bf16[4,2,49152]{2,1,0:T(2,128)(2,1)}), bf16[4,2,49152]{2,1,0:T(2,128)(2,1)S(1)}, u32[]{:S(2)}, u32[]{:S(2)}) async-start(bf16[4,2,49152]{2,1,0:T(2,128)(2,1)} %reshape.507), calls=%async_computation.4 | async-start | bytes 1572864 | tf_op jit(solution)/shard_map/all_to_all | solution.py:160
  91.0 12.8 %copy-start.93 = (f32[768]{0:T(1024)}, f32[768]{0:T(1024)S(1)}, u32[]{:S(2)}) copy-start(f32[768]{0:T(1024)S(1)} %get-tuple-element.241) | copy-start | bytes 9220
  91.0 40.6 %copy-start.82 = (f32[1,192]{1,0:T(1,128)}, f32[1,192]{1,0:T(1,128)S(1)}, u32[]{:S(2)}) copy-start(f32[1,192]{1,0:T(1,128)S(1)} %get-tuple-element.289) | copy-start | bytes 2308
  103.8 15.9 %copy-start.47 = (bf16[24,8,4,512]{3,1,2,0:T(8,128)(2,1)}, bf16[24,8,4,512]{3,1,2,0:T(8,128)(2,1)S(1)}, u32[]{:S(2)}) copy-start(bf16[24,8,4,512]{3,1,2,0:T(8,128)(2,1)S(1)} %copy.218) | copy-start | bytes 2359300
  103.8 15.9 %copy-start.107 = (bf16[2,1,768,192]{2,3,1,0:T(8,128)(2,1)S(1)}, bf16[2,1,768,192]{2,3,1,0:T(8,128)(2,1)}, u32[]{:S(2)}) copy-start(bf16[2,1,768,192]{2,3,1,0:T(8,128)(2,1)} %param.26) | copy-start | bytes 1769476
  121.4 17.4 %copy-start.16 = (f32[2048,192]{0,1:T(8,128)}, f32[2048,192]{0,1:T(8,128)S(1)}, u32[]{:S(2)}) copy-start(f32[2048,192]{0,1:T(8,128)S(1)} %get-tuple-element.300) | copy-start | bytes 4718596
  133.6 15.1 %all-to-all-start.5 = ((bf16[4,512,192]{1,2,0:T(8,128)(2,1)}), bf16[4,512,192]{1,2,0:T(8,128)(2,1)S(1)}, u32[]{:S(2)}, u32[]{:S(2)}) async-start(bf16[4,512,192]{1,2,0:T(8,128)(2,1)} %bitcast.406), calls=%async_computation.5 | async-start | bytes 1572864 | tf_op jit(solution)/shard_map/all_to_all | solution.py:140
  148.7 15.5 %all-to-all-start.8 = ((bf16[4,512,192]{1,2,0:T(8,128)(2,1)}), bf16[4,512,192]{1,2,0:T(8,128)(2,1)S(1)}, u32[]{:S(2)}, u32[]{:S(2)}) async-start(bf16[4,512,192]{1,2,0:T(8,128)(2,1)} %bitcast.403), calls=%async_computation.8 | async-start | bytes 1572864 | tf_op jit(solution)/shard_map/all_to_all | solution.py:138
  164.2 19.4 %copy-start.34 = (bf16[4,512,192]{1,2,0:T(8,128)(2,1)}, bf16[4,512,192]{1,2,0:T(8,128)(2,1)S(1)}, u32[]{:S(2)}) copy-start(bf16[4,512,192]{1,2,0:T(8,128)(2,1)S(1)} %all-to-all-done.8) | copy-start | bytes 2359300
  164.2 15.9 %all-to-all-start.7 = ((bf16[4,512,192]{1,2,0:T(8,128)(2,1)}), bf16[4,512,192]{1,2,0:T(8,128)(2,1)}, u32[]{:S(2)}, u32[]{:S(2)}) async-start(bf16[4,512,192]{1,2,0:T(8,128)(2,1)} %bitcast.404), calls=%async_computation.7 | async-start | bytes 1572864 | tf_op jit(solution)/shard_map/all_to_all | solution.py:137
  180.2 15.1 %all-to-all-start.6 = ((bf16[4,512,192]{1,2,0:T(8,128)(2,1)}), bf16[4,512,192]{1,2,0:T(8,128)(2,1)S(1)}, u32[]{:S(2)}, u32[]{:S(2)}) async-start(bf16[4,512,192]{1,2,0:T(8,128)(2,1)} %bitcast.405), calls=%async_computation.6 | async-start | bytes 1572864 | tf_op jit(solution)/shard_map/all_to_all | solution.py:139
  213.9 6.6 copy-start.42
  216.3 15.9 %all-to-all-start.9 = ((bf16[4,2,49152]{2,1,0:T(2,128)(2,1)}), bf16[4,2,49152]{2,1,0:T(2,128)(2,1)}, u32[]{:S(2)}, u32[]{:S(2)}) async-start(bf16[4,2,49152]{2,1,0:T(2,128)(2,1)} %reshape.509), calls=%async_computation.9 | async-start | bytes 1572864 | tf_op jit(solution)/shard_map/all_to_all | solution.py:160
  221.9 45.1 %copy-start.14 = (f32[4,24,8,512]{3,2,0,1:T(8,128)}, f32[4,24,8,512]{3,2,0,1:T(8,128)S(1)}, u32[]{:S(2)}) copy-start(f32[4,24,8,512]{3,2,0,1:T(8,128)S(1)} %copy.217) | copy-start | bytes 4718596
  238.5 15.9 %copy-start.48 = (bf16[24,8,4,512]{3,1,2,0:T(8,128)(2,1)}, bf16[24,8,4,512]{3,1,2,0:T(8,128)(2,1)S(1)}, u32[]{:S(2)}) copy-start(bf16[24,8,4,512]{3,1,2,0:T(8,128)(2,1)S(1)} %copy.219) | copy-start | bytes 2359300
  238.5 15.9 %copy-start.102 = (f32[1,192]{1,0:T(1,128)S(1)}, f32[1,192]{1,0:T(1,128)}, u32[]{:S(2)}) copy-start(f32[1,192]{1,0:T(1,128)} %get-tuple-element.292) | copy-start | bytes 2308
  238.5 15.9 %copy-start.108 = (bf16[2,1,768,192]{2,3,1,0:T(8,128)(2,1)S(1)}, bf16[2,1,768,192]{2,3,1,0:T(8,128)(2,1)}, u32[]{:S(2)}) copy-start(bf16[2,1,768,192]{2,3,1,0:T(8,128)(2,1)} %param.26) | copy-start | bytes 1769476
  256.7 23.1 %copy-start.98 = (f32[1,192]{1,0:T(1,128)S(1)}, f32[1,192]{1,0:T(1,128)}, u32[]{:S(2)}) copy-start(f32[1,192]{1,0:T(1,128)} %get-tuple-element.290) | copy-start | bytes 2308
  283.9 6.3 copy-start.68
  292.9 15.9 %all-to-all-start.10 = ((bf16[4,512,192]{1,2,0:T(8,128)(2,1)}), bf16[4,512,192]{1,2,0:T(8,128)(2,1)}, u32[]{:S(2)}, u32[]{:S(2)}) async-start(bf16[4,512,192]{1,2,0:T(8,128)(2,1)} %bitcast.474), calls=%async_computation.10 | async-start | bytes 1572864 | tf_op jit(solution)/shard_map/all_to_all | solution.py:256
  322.4 6.9 copy-start.63
  339.2 26.2 %all-to-all-start.13 = ((bf16[4,2,49152]{2,1,0:T(2,128)(2,1)}), bf16[4,2,49152]{2,1,0:T(2,128)(2,1)S(1)}, u32[]{:S(2)}, u32[]{:S(2)}) async-start(bf16[4,2,49152]{2,1,0:T(2,128)(2,1)} %reshape.517), calls=%async_computation.13 | async-start | bytes 1572864 | tf_op jit(solution)/shard_map/all_to_all | solution.py:284
  343.1 11.6 %copy-start.26 = (bf16[512,768]{1,0:T(8,128)(2,1)S(1)}, bf16[512,768]{1,0:T(8,128)(2,1)}, u32[]{:S(2)}) copy-start(bf16[512,768]{1,0:T(8,128)(2,1)} %copy-done.25) | copy-start | bytes 2359300
  365.3 14.0 %copy-start.43 = (bf16[4,2,49152]{2,1,0:T(2,128)(2,1)}, bf16[4,2,49152]{2,1,0:T(2,128)(2,1)S(1)}, u32[]{:S(2)}) copy-start(bf16[4,2,49152]{2,1,0:T(2,128)(2,1)S(1)} %all-to-all-done.13) | copy-start | bytes 2359300
  365.3 27.9 %all-to-all-start.14 = ((bf16[4,2,49152]{2,1,0:T(2,128)(2,1)}), bf16[4,2,49152]{2,1,0:T(2,128)(2,1)}, u32[]{:S(2)}, u32[]{:S(2)}) async-start(bf16[4,2,49152]{2,1,0:T(2,128)(2,1)} %reshape.511), calls=%async_computation.14 | async-start | bytes 1572864 | tf_op jit(solution)/shard_map/all_to_all | solution.py:285
  385.4 12.3 %copy-start.75 = (f32[768]{0:T(1024)S(1)}, f32[768]{0:T(1024)}, u32[]{:S(2)}) copy-start(f32[768]{0:T(1024)} %copy-done.74) | copy-start | bytes 9220
  385.4 12.4 %copy-start.35 = (bf16[4,512,192]{1,2,0:T(8,128)(2,1)S(1)}, bf16[4,512,192]{1,2,0:T(8,128)(2,1)}, u32[]{:S(2)}) copy-start(bf16[4,512,192]{1,2,0:T(8,128)(2,1)} %copy-done.34) | copy-start | bytes 2359300
  393.3 18.6 %all-to-all-start.12 = ((bf16[4,2,49152]{2,1,0:T(2,128)(2,1)}), bf16[4,2,49152]{2,1,0:T(2,128)(2,1)}, u32[]{:S(2)}, u32[]{:S(2)}) async-start(bf16[4,2,49152]{2,1,0:T(2,128)(2,1)} %reshape.515), calls=%async_computation.12 | async-start | bytes 1572864 | tf_op jit(solution)/shard_map/all_to_all | solution.py:283
  411.8 22.0 %all-to-all-start.11 = ((bf16[4,2,49152]{2,1,0:T(2,128)(2,1)}), bf16[4,2,49152]{2,1,0:T(2,128)(2,1)}, u32[]{:S(2)}, u32[]{:S(2)}) async-start(bf16[4,2,49152]{2,1,0:T(2,128)(2,1)} %reshape.513), calls=%async_computation.11 | async-start | bytes 1572864 | tf_op jit(solution)/shard_map/all_to_all | solution.py:282
  441.0 13.9 %copy-start.94 = (f32[768]{0:T(1024)S(1)}, f32[768]{0:T(1024)}, u32[]{:S(2)}) copy-start(f32[768]{0:T(1024)} %copy-done.93) | copy-start | bytes 9220
  441.0 13.9 %copy-start.109 = (bf16[2,1,768,192]{2,3,1,0:T(8,128)(2,1)S(1)}, bf16[2,1,768,192]{2,3,1,0:T(8,128)(2,1)}, u32[]{:S(2)}) copy-start(bf16[2,1,768,192]{2,3,1,0:T(8,128)(2,1)} %param.26) | copy-start | bytes 1769476
  454.9 6.3 copy-start.10
  463.9 16.5 %all-to-all-start.15 = ((bf16[4,512,192]{1,2,0:T(8,128)(2,1)}), bf16[4,512,192]{1,2,0:T(8,128)(2,1)}, u32[]{:S(2)}, u32[]{:S(2)}) async-start(bf16[4,512,192]{1,2,0:T(8,128)(2,1)} %bitcast.473), calls=%async_computation.15 | async-start | bytes 1572864 | tf_op jit(solution)/shard_map/all_to_all | solution.py:256
  476.6 9.8 %copy-start.5 = (f32[512,768]{1,0:T(8,128)S(1)}, f32[512,768]{1,0:T(8,128)}, u32[]{:S(2)}) copy-start(f32[512,768]{1,0:T(8,128)} %copy-done.4) | copy-start | bytes 4718596
  476.6 9.8 %copy-start.77 = (f32[512]{0:T(512)S(1)}, f32[512]{0:T(512)}, u32[]{:S(2)}) copy-start(f32[512]{0:T(512)} %copy-done.76) | copy-start | bytes 6148
  476.6 9.8 %copy-start.79 = (f32[512]{0:T(512)S(1)}, f32[512]{0:T(512)}, u32[]{:S(2)}) copy-start(f32[512]{0:T(512)} %copy-done.78) | copy-start | bytes 6148
  489.5 6.7 copy-start.61
  512.8 29.3 %all-to-all-start.18 = ((bf16[4,2,49152]{2,1,0:T(2,128)(2,1)}), bf16[4,2,49152]{2,1,0:T(2,128)(2,1)}, u32[]{:S(2)}, u32[]{:S(2)}) async-start(bf16[4,2,49152]{2,1,0:T(2,128)(2,1)} %reshape.525), calls=%async_computation.18 | async-start | bytes 1572864 | tf_op jit(solution)/shard_map/all_to_all | solution.py:284
  530.6 8.0 copy-start.29
  538.6 8.1 copy-start.20
  542.1 26.1 %all-to-all-start.17 = ((bf16[4,2,49152]{2,1,0:T(2,128)(2,1)}), bf16[4,2,49152]{2,1,0:T(2,128)(2,1)}, u32[]{:S(2)}, u32[]{:S(2)}) async-start(bf16[4,2,49152]{2,1,0:T(2,128)(2,1)} %reshape.523), calls=%async_computation.17 | async-start | bytes 1572864 | tf_op jit(solution)/shard_map/all_to_all | solution.py:283
  546.3 160.5 %all-reduce.10.cloned.1.call-start = ((), (), s32[]{:S(2)}) async-start(), calls=%async_computation.20 | async-start | bytes 9437184 | tf_op jit(solution)/shard_map/psum | solution.py:387
  558.3 14.1 %copy-start.9 = (bf16[2048,768]{1,0:T(8,128)(2,1)S(1)}, bf16[2048,768]{1,0:T(8,128)(2,1)}, u32[]{:S(2)}) copy-start(bf16[2048,768]{1,0:T(8,128)(2,1)} %copy-done.8) | copy-start | bytes 9437188
  568.2 19.8 %all-to-all-start.16 = ((bf16[4,2,49152]{2,1,0:T(2,128)(2,1)}), bf16[4,2,49152]{2,1,0:T(2,128)(2,1)}, u32[]{:S(2)}, u32[]{:S(2)}) async-start(bf16[4,2,49152]{2,1,0:T(2,128)(2,1)} %reshape.521), calls=%async_computation.16 | async-start | bytes 1572864 | tf_op jit(solution)/shard_map/all_to_all | solution.py:282
  572.4 268.4 %all-reduce.12.cloned.1.call-start = ((), (), s32[]{:S(2)}) async-start(), calls=%async_computation.21 | async-start | bytes 6684672 | tf_op jit(solution)/shard_map/psum | solution.py:374
  601.5 12.9 %copy-start.91 = (f32[192]{0:T(256)S(1)}, f32[192]{0:T(256)}, u32[]{:S(2)}) copy-start(f32[192]{0:T(256)} %get-tuple-element.234) | copy-start | bytes 2308
  601.5 12.9 %copy-start.97 = (f32[192]{0:T(256)S(1)}, f32[192]{0:T(256)}, u32[]{:S(2)}) copy-start(f32[192]{0:T(256)} %get-tuple-element.273) | copy-start | bytes 2308
  610.2 51.7 %all-to-all-start.19 = ((bf16[4,2,49152]{2,1,0:T(2,128)(2,1)}), bf16[4,2,49152]{2,1,0:T(2,128)(2,1)}, u32[]{:S(2)}, u32[]{:S(2)}) async-start(bf16[4,2,49152]{2,1,0:T(2,128)(2,1)} %reshape.519), calls=%async_computation.19 | async-start | bytes 1572864 | tf_op jit(solution)/shard_map/all_to_all | solution.py:285
  (69 other events, 193.7 us)
Sparse Core Ops, SparseCore 0:
  553.4 147.8 all-reduce.9
  706.9 133.8 all-reduce.11
where the time goes:
time: 868 us; the launch traced here: 858 us
  waiting for transfers between devices  219 us (25%)
  matrix products  161 us (19%)
  local copies, waits for them, and re-layouts  131 us (15%)
  blocking collectives  128 us (15%)
  other arithmetic  121 us (14%)
  starting transfers between devices  81.9 us (9%)
  between operations  16.3 us (2%)
    psum x1, waiting for transfers between devices, shards(): lax.psum((stacked[0], stacked[1], stacked[6], stacked[7], stacked[8], sta...  134 us
    unnamed x270, local copies, waits for them, and re-layouts  76.2 us
    unnamed x11, other arithmetic  62.1 us
    psum x1, blocking collectives, shards(): lax.psum((stacked[2], stacked[3], stacked[4], stacked[5]), ('dp', 'grp'))  47.3 us
    psum x1, blocking collectives, shards(): lax.psum((stacked[0], stacked[1], stacked[6], stacked[7], stacked[8], sta...  37.9 us
    dot_general x2, matrix products, layer_forward(): jnp.dot(group_rows, widen_weight[layer_params, 0], preferred_element_type...  31.7 us
    psum x2, blocking collectives, layer_backward(): total_sum, total_cross = lax.psum((part_sum, part_cross), 'grp')  22.2 us
    sub x2, matrix products, single(): expon = jnp.exp(scores - highest)  21.1 us
  transfers between devices with their start and end apart: 22, of which 13 were waited for; matrix products, arithmetic and copies ran while one was open for 25% of the time, Pallas kernels for 0%

commit v1 on v0

v1 whole, which is shorter than its diff:
```python
import functools
import math

import jax
import jax.numpy as jnp
from jax import lax
from jax.experimental import pallas as pl
from jax.experimental.pallas import tpu as pltpu
from jax.sharding import PartitionSpec as P

HEAD = 64
EPSILON = 1e-05
MASKED = -1e30
F32 = jnp.float32
BF16 = jnp.bfloat16
MESH = pl.DeviceIdType.MESH
NN = (((1,), (0,)), ((), ()))
NT = (((1,), (1,)), ((), ()))
ONES = 16


def mm(left, right, dims=NN):
    return lax.dot_general(left, right, dims, preferred_element_type=F32)


def lanes(block):
    total = block[:, 0:128]
    for start in range(128, block.shape[1], 128):
        total = total + block[:, start : start + 128]
    return total


def pack(first, second):
    pieces = []
    for row in (first, second):
        pieces += [row[:, start : start + 128] for start in range(0, row.shape[1], 128)]
    return jnp.concatenate(pieces, axis=0)


def unpack(tile):
    return jnp.concatenate([tile[k : k + 1] for k in range(tile.shape[0])], axis=1)


def phi_of(u):
    return 0.5 * (1.0 + lax.erf(u * (1.0 / math.sqrt(2.0))))


def body(
    depth,
    seqs,
    ndp,
    ngrp,
    tokens,
    gc,
    fc,
    part_rows,
    lens,
    x_hbm,
    ct,
    tw,
    tb,
    wo_hbm,
    bo,
    fg,
    fs,
    ww,
    bw,
    ws,
    nb,
    sg,
    ss,
    ytok,
    gx_hbm,
    grads_hbm,
    wog_hbm,
    vec_hbm,
    xT,
    qkT,
    vtok,
    eT,
    rls,
    og,
    oown,
    xh1,
    inv1,
    hT,
    xh2,
    inv2,
    twT,
    wkp,
    wvp,
    vrow,
    wwT,
    wsT,
    woT,
    wog,
    cola,
    colb,
    rowa,
    qz,
    kmb,
    vaug,
    goz,
    abuf,
    gub,
    ghs,
    gqkv,
    r1s,
    r2s,
    gy,
    gxs,
    accw,
    accs,
    acco,
    acct,
    accv,
    vec8,
    gbuf,
    rsbuf,
    stat_out,
    stat_in,
    local_sem,
    gx_sem,
    send_own,
    send_pair,
    send_relay,
    recv_far,
    recv_pair,
    recv_relay,
    stat_send,
    stat_recv,
    rs_send,
    rs_recv,
    ag_send,
    ag_recv,
    ag_own,
    fin_own,
    fin_send,
    fin_recv,
):
    heads = gc // HEAD
    items = depth * seqs
    width = gc * ngrp
    chunk = part_rows // ndp
    half = tokens // 128
    dp = lax.axis_index("dp")
    g = lax.axis_index("grp")
    pair, far = g ^ 1, g ^ 2
    near_far = g ^ 3

    barrier = pltpu.get_barrier_semaphore()

    def greet(k, carry):
        pl.semaphore_signal(barrier, inc=1, device_id=(lax.rem(dp + k, ndp), g), device_id_type=MESH)
        return carry

    lax.fori_loop(1, ndp, greet, 0)
    for other in (pair, far, near_far):
        pl.semaphore_signal(barrier, inc=1, device_id=(dp, other), device_id_type=MESH)

    wo_copies = []
    for l in range(depth):
        for part in range(2):
            wo_copies.append(
                pltpu.make_async_copy(
                    wo_hbm.at[l, pl.ds(part * (width // 2), width // 2), :],
                    gbuf.at[2 * l + part, pl.ds(0, width // 2), :],
                    local_sem.at[2 * l + part],
                )
            )
            wo_copies[-1].start()
    x_copy = pltpu.make_async_copy(x_hbm, ytok, local_sem.at[2 * depth])
    x_copy.start()
    own_copies = []
    for l in range(depth):
        own_copies.append(
            pltpu.make_async_copy(
                wo_hbm.at[l, pl.ds(pl.multiple_of(g * gc, 64), gc), :],
                wog.at[l],
                local_sem.at[2 * depth + 1 + l],
            )
        )
        own_copies[-1].start()

    lane = lax.broadcasted_iota(jnp.int32, (1, 128), 1)
    for l in range(depth):
        twT[l] = tw[l].T
        wwT[l] = ww[l].T
        wsT[l] = ws[l].T
        wkp[l] = jnp.zeros(wkp.shape[1:], BF16)
        wvp[l] = jnp.zeros(wvp.shape[1:], BF16)
        vrow[l] = jnp.zeros(vrow.shape[1:], F32)
        for h in range(heads):
            wkp[l, :, h * 128 : h * 128 + HEAD] = tw[l, :, gc + h * HEAD : gc + (h + 1) * HEAD]
            wvp[l, :, h * 128 : h * 128 + HEAD] = tw[
                l, :, 2 * gc + h * HEAD : 2 * gc + (h + 1) * HEAD
            ]
            vrow[l, 0:1, h * 128 : (h + 1) * 128] = jnp.where(
                (lane == HEAD) | (lane == HEAD + 1), 1.0, 0.0
            )
            vrow[l, 0:1, h * 128 : h * 128 + HEAD] = tb[l, 1:2, h * HEAD : (h + 1) * HEAD]
        rowa[...] = jnp.zeros(rowa.shape, F32)
        rowa[0:1] = bo[l : l + 1]
        rowa[1:2] = fg[l : l + 1]
        rowa[2:3] = fs[l : l + 1]
        rowa[3:4] = bw[l : l + 1]
        cola[l] = rowa[...].T
        rowa[0:2, 0:gc] = tb[l]
        rowa[2:3, 0:gc] = nb[l : l + 1]
        rowa[3:4, 0:gc] = sg[l : l + 1]
        rowa[4:5, 0:gc] = ss[l : l + 1]
        colb[l] = rowa[:, 0:gc].T
    ones_rows = jnp.ones((ONES, tokens), BF16)
    for i in range(items):
        xT[i, gc : gc + ONES] = ones_rows
        hT[i, gc : gc + ONES] = ones_rows
        oown[i, gc : gc + ONES] = ones_rows
    row = lax.broadcasted_iota(jnp.int32, (HEAD, tokens), 0)
    for h in range(heads):
        qz[h, HEAD : 2 * HEAD] = jnp.where(row == 0, 1.0, 0.0).astype(BF16)
        goz[h, HEAD : 2 * HEAD] = jnp.zeros((HEAD, tokens), BF16)
        vaug[h, HEAD : HEAD + ONES] = ones_rows
    x_copy.wait()
    for s in range(seqs):
        xT[s, 0:gc] = ytok[s].T
    for copy in wo_copies:
        copy.wait()
    for copy in own_copies:
        copy.wait()
    for l in range(depth):
        for j in range(ngrp):

            @pl.when(g == j)
            def _(l=l, j=j):
                for part in range(2):
                    woT[l, :, part * (width // 2) : (part + 1) * (width // 2)] = gbuf[
                        2 * l + part, 0 : width // 2, j * gc : (j + 1) * gc
                    ].T

    pl.semaphore_wait(barrier, ndp - 1 + 3)

    def block_of(i, owner):
        return og.at[i, pl.ds(pl.multiple_of(owner * gc, 64), gc), :]

    def to_pair(i, p):
        return pltpu.make_async_remote_copy(
            block_of(i, g), block_of(i, g), send_pair.at[p, i], recv_pair.at[p, i], (dp, pair), device_id_type=MESH
        )

    def to_far(i, p):
        return pltpu.make_async_remote_copy(
            block_of(i, g), block_of(i, g), send_own.at[p, i], recv_far.at[p, i], (dp, far), device_id_type=MESH
        )

    def relay(i, p):
        return pltpu.make_async_remote_copy(
            block_of(i, far), block_of(i, far), send_relay.at[p, i], recv_relay.at[p, i], (dp, pair), device_id_type=MESH
        )

    def send_block(i, p):
        to_far(i, p).start()
        to_pair(i, p).start()

    def relay_block(i, p):
        to_far(i, p).wait_recv()
        relay(i, p).start()

    def finish_block(i, p):
        to_pair(i, p).wait()
        relay(i, p).wait()
        to_far(i, p).wait_send()

    def stat_copy(kind, i, k):
        other = g ^ (k + 1)
        return pltpu.make_async_remote_copy(
            stat_out.at[kind, i],
            stat_in.at[kind, i, k],
            stat_send.at[kind, i],
            stat_recv.at[kind, i],
            (dp, other),
            device_id_type=MESH,
        )

    def send_stats(kind, i, first, second):
        stat_out[kind, i] = pack(first, second)
        for k in range(ngrp - 1):
            stat_copy(kind, i, k).start()

    def wait_stats(kind, i):
        every = stat_in.at[kind, i]
        pltpu.make_async_copy(every, every, stat_recv.at[kind, i]).wait()
        pltpu.make_async_copy(every, every, stat_send.at[kind, i]).wait()
        return [stat_out[kind, i]] + [stat_in[kind, i, k] for k in range(ngrp - 1)]

    def moments(tiles):
        mean = (tiles[0][:half] + tiles[1][:half] + tiles[2][:half] + tiles[3][:half]) * (1.0 / ngrp)
        second = tiles[0][half:] + tiles[1][half:] + tiles[2][half:] + tiles[3][half:]
        for tile in tiles:
            off = tile[:half] - mean
            second = second + gc * (off * off)
        inverse = lax.rsqrt(second * (1.0 / width) + EPSILON)
        return unpack(mean), unpack(inverse)

    def two_means(tiles):
        total = (tiles[0] + tiles[1] + tiles[2] + tiles[3]) * (1.0 / width)
        return unpack(total[:half]), unpack(total[half:])

    def local_moments(rows):
        mean = jnp.sum(rows, axis=0, keepdims=True) * (1.0 / gc)
        off = rows - mean
        return mean, jnp.sum(off * off, axis=0, keepdims=True)

    def own(l, k):
        return cola[l, pl.ds(pl.multiple_of(g * gc, 64), gc), k : k + 1]

    def attend(i):
        l = i // seqs
        s = i - l * seqs
        length = lens[s]
        xt = xT[i, 0:gc]
        qf = mm(twT[l, 0:gc], xt) + colb[l, :, 0:1]
        q = qf.astype(BF16) * jnp.asarray(HEAD ** (-0.5), BF16)
        qkT[i, 0:gc] = q
        for h in range(heads):
            qz[h, 0:HEAD] = q[h * HEAD : (h + 1) * HEAD]
        qkT[i, gc : 2 * gc] = mm(twT[l, gc : 2 * gc], xt).astype(BF16)
        v = (mm(twT[l, 2 * gc : 3 * gc], xt) + colb[l, :, 1:2]).astype(BF16)
        for h in range(heads):
            vaug[h, 0:HEAD] = v[h * HEAD : (h + 1) * HEAD]
        xk = ytok[s]
        key = lax.broadcasted_iota(jnp.int32, (tokens, 128), 0)
        spot = lax.broadcasted_iota(jnp.int32, (tokens, 128), 1)
        hide = jnp.where((key >= length) & (spot == HEAD), MASKED, 0.0)
        for h in range(heads):
            cols = slice(h * 128, (h + 1) * 128)
            kmb[h] = (mm(xk, wkp[l, :, cols]) + hide).astype(BF16)
            vtok[i, h] = (mm(xk, wvp[l, :, cols]) + vrow[l, 0:1, cols]).astype(BF16)

        def head(h, carry):
            st = mm(kmb[h], qz[h])
            top = jnp.max(st, axis=0, keepdims=True)
            e = jnp.exp(st - top).astype(BF16)
            eT[i * heads + h] = e
            ot = mm(vaug[h], e)
            rl = 1.0 / ot[HEAD : HEAD + 1]
            rls[i * heads + h] = rl
            o = (ot[0:HEAD] * rl).astype(BF16)
            oown[i, pl.ds(pl.multiple_of(h * HEAD, 64), HEAD)] = o
            og[i, pl.ds(pl.multiple_of(g * gc + h * HEAD, 64), HEAD)] = o
            return carry

        lax.fori_loop(0, heads, head, 0)
        send_block(i, 0)

    def mix(i):
        l = i // seqs
        finish_block(i, 0)
        r1 = xT[i, 0:gc].astype(F32) + mm(woT[l], og[i]) + own(l, 0)
        r1s[...] = r1
        send_stats(0, i, *local_moments(r1))

    def feed(i):
        l = i // seqs
        mean, inverse = moments(wait_stats(0, i))
        xhat = (r1s[...] - mean) * inverse
        xh1[i] = xhat.astype(BF16)
        inv1[i] = inverse
        h = (xhat * own(l, 1) + own(l, 2)).astype(BF16)
        hT[i, 0:gc] = h
        for c in range(0, fc, 128):
            u = mm(wwT[l, c : c + 128], h) + cola[l, c : c + 128, 3:4]
            abuf[c : c + 128] = (u * phi_of(u)).astype(BF16)
        r2 = h.astype(F32) + mm(wsT[l], abuf[...]) + colb[l, :, 2:3]
        r2s[i % 2] = r2
        send_stats(1, i, *local_moments(r2))

    def close(i):
        l = i // seqs
        s = i - l * seqs
        mean, inverse = moments(wait_stats(1, i))
        xhat = (r2s[i % 2] - mean) * inverse
        xh2[i] = xhat.astype(BF16)
        inv2[i] = inverse
        y = (xhat * colb[l, :, 3:4] + colb[l, :, 4:5]).astype(BF16)
        ytok[s] = y.T

        @pl.when(l < depth - 1)
        def _():
            xT[jnp.minimum(i + seqs, items - 1), 0:gc] = y

    def place(j):
        l = depth - 1 - j // seqs
        s = j % seqs
        return l, s, l * seqs + s

    def back_open(j):
        l, s, i = place(j)

        @pl.when(l == depth - 1)
        def _():
            gy[s] = ct[s].T.astype(F32)

        @pl.when(s == 0)
        def _():
            for k in range(accv.shape[1]):
                accv[l, k] = jnp.zeros(accv.shape[2:], F32)

        grad = gy[s]
        xhat = xh2[i].astype(F32)
        t = grad * colb[l, :, 3:4]
        accv[l, 0] += lanes(grad * xhat)
        accv[l, 1] += lanes(grad)
        send_stats(
            2, i, jnp.sum(t, axis=0, keepdims=True), jnp.sum(t * xhat, axis=0, keepdims=True)
        )

    def back_feed(j):
        l, s, i = place(j)

        @pl.when(s == 0)
        def _():
            accw[...] = jnp.zeros(accw.shape, F32)
            accs[...] = jnp.zeros(accs.shape, F32)

        mean_t, mean_x = two_means(wait_stats(2, i))
        t = gy[s] * colb[l, :, 3:4]
        g2 = inv2[i] * (t - mean_t - xh2[i].astype(F32) * mean_x)
        gf = g2.astype(BF16)
        accv[l, 2] += lanes(gf.astype(F32))
        h = hT[i, 0:gc]
        for c in range(0, fc, 128):
            u = mm(wwT[l, c : c + 128], h) + cola[l, c : c + 128, 3:4]
            big = phi_of(u)
            abuf[c : c + 128] = (u * big).astype(BF16)
            slope = big + u * jnp.exp(-0.5 * u * u) * (1.0 / math.sqrt(2.0 * math.pi))
            gub[c : c + 128] = (mm(ws[l, c : c + 128], gf) * slope).astype(BF16)
        accs[...] += mm(gf, abuf[...], NT)
        accw[...] += mm(hT[i], gub[...], NT)
        gh = (g2 + mm(ww[l], gub[...])).astype(BF16)
        ghs[...] = gh
        ghf = gh.astype(F32)
        xhat = xh1[i].astype(F32)
        accv[l, 3] += lanes(ghf * xhat)
        accv[l, 4] += lanes(ghf)
        t1 = ghf * own(l, 1)
        send_stats(
            3, i, jnp.sum(t1, axis=0, keepdims=True), jnp.sum(t1 * xhat, axis=0, keepdims=True)
        )

    def back_norm(j):
        l, s, i = place(j)
        mean_t, mean_x = two_means(wait_stats(3, i))
        t1 = ghs[...].astype(F32) * own(l, 1)
        g1 = inv1[i] * (t1 - mean_t - xh1[i].astype(F32) * mean_x)
        og[i, pl.ds(pl.multiple_of(g * gc, 64), gc)] = g1.astype(BF16)
        send_block(i, 1)

    def gx_copy(s):
        return pltpu.make_async_copy(gxs.at[s % 2], gx_hbm.at[s], gx_sem.at[s % 2])

    def back_attend(j):
        l, s, i = place(j)
        finish_block(i, 1)

        @pl.when(s == 0)
        def _():
            acco[...] = jnp.zeros(acco.shape, F32)
            acct[...] = jnp.zeros(acct.shape, F32)

        acco[...] += mm(oown[i], og[i], NT)
        go = mm(wog[l], og[i]).astype(BF16)
        for h in range(heads):
            goz[h, 0:HEAD] = go[h * HEAD : (h + 1) * HEAD]
        edge = lax.broadcasted_iota(jnp.int32, (ONES, tokens), 0)

        def head(h, carry):
            base = pl.multiple_of(h * HEAD, 64)
            gos = (goz[h, 0:HEAD].astype(F32) * rls[i * heads + h]).astype(BF16)
            delta = jnp.sum(
                gos.astype(F32) * oown[i, pl.ds(base, HEAD)].astype(F32), axis=0, keepdims=True
            )
            high = delta.astype(BF16).astype(F32)
            goz[h, 0:HEAD] = gos
            goz[h, HEAD : HEAD + ONES] = jnp.where(
                edge == 0, -high, jnp.where(edge == 1, high - delta, 0.0)
            ).astype(BF16)
            e = eT[i * heads + h]
            gs = (e.astype(F32) * mm(vtok[i, h], goz[h])).astype(BF16)
            gqkv[pl.ds(base, HEAD)] = (
                mm(qkT[i, pl.ds(pl.multiple_of(gc + h * HEAD, 64), HEAD)], gs) * HEAD ** (-0.5)
            ).astype(BF16)
            gqkv[pl.ds(pl.multiple_of(gc + h * HEAD, 64), HEAD)] = mm(
                qkT[i, pl.ds(base, HEAD)], gs, NT
            ).astype(BF16)
            gqkv[pl.ds(pl.multiple_of(2 * gc + h * HEAD, 64), HEAD)] = mm(gos, e, NT).astype(BF16)
            return carry

        lax.fori_loop(0, heads, head, 0)
        acct[...] += mm(xT[i], gqkv[...], NT)
        gx = mm(tw[l], gqkv[...]) + og[i, pl.ds(pl.multiple_of(g * gc, 64), gc)].astype(F32)

        @pl.when(l > 0)
        def _():
            gy[s] = gx

        @pl.when(l == 0)
        def _():
            @pl.when(s >= 2)
            def _():
                gx_copy(s).wait()

            gxs[s % 2] = gx.T
            gx_copy(s).start()

    def pack_feed(l):
        gbuf[2 * l, 0:gc] = accw[0:gc].astype(BF16)
        gbuf[2 * l, gc : 2 * gc] = accs[...].astype(BF16)
        vec8[l, 0:1] = accw[gc : gc + 1]

    def pack_attend(l):
        q = 2 * l + 1
        gbuf[q, 0:gc] = acco[0:gc].astype(BF16)
        gbuf[q, gc : 2 * gc, 0 : 3 * gc] = acct[0:gc].astype(BF16)
        vec8[l, 1:2] = acco[gc : gc + 1]
        vec8[l, 2:8] = jnp.zeros((6, width), F32)
        vec8[l, 2:3, 0 : 3 * gc] = acct[gc : gc + 1]
        for k in range(accv.shape[1]):
            vec8[l, 3 + k : 4 + k, 0:gc] = jnp.sum(accv[l, k].T, axis=0, keepdims=True)
        vec = vec8[l]
        for k in range(0, width // 128, 2):
            both = jnp.concatenate(
                [vec[:, k * 128 : (k + 1) * 128], vec[:, (k + 1) * 128 : (k + 2) * 128]], axis=0
            )
            gbuf[q, gc + 8 * k : gc + 8 * k + 16, width - 128 : width] = both.astype(BF16)

    def rows_of(q, owner):
        return gbuf.at[q, pl.ds(pl.multiple_of(owner * chunk, 16), chunk), :]

    def summed_rows(q):
        return grads_hbm.at[q, pl.ds(pl.multiple_of(dp * chunk, 16), chunk), :]

    def scatter_copy(q, k):
        to = lax.rem(dp + k, ndp)
        return pltpu.make_async_remote_copy(
            rows_of(q, to), rsbuf.at[q % 2, k - 1], rs_send.at[q], rs_recv.at[q], (to, g), device_id_type=MESH
        )

    def gather_copy(q, k):
        to = lax.rem(dp + k, ndp)
        return pltpu.make_async_remote_copy(
            rows_of(q, dp), summed_rows(q), ag_send.at[q], ag_recv.at[q], (to, g), device_id_type=MESH
        )

    def own_rows(q):
        return pltpu.make_async_copy(rows_of(q, dp), summed_rows(q), ag_own.at[q])

    def start_all(copy, q):
        def step(k, carry):
            copy(q, k).start()
            return carry

        lax.fori_loop(1, ndp, step, 0)

    def wait_all(sem, q):
        every = rsbuf.at[q % 2]
        pltpu.make_async_copy(every, every, sem.at[q]).wait()

    def reduce_part(q):
        wait_all(rs_recv, q)
        wait_all(rs_send, q)
        mine = pl.ds(pl.multiple_of(dp * chunk, 16), chunk)

        def add(k, total):
            return total + rsbuf[q % 2, k].astype(F32)

        total = lax.fori_loop(0, ndp - 1, add, gbuf[q, mine].astype(F32))
        gbuf[q, mine] = total.astype(BF16)
        start_all(gather_copy, q)
        own_rows(q).start()

    def gathered_part(q):
        own_rows(q).wait()
        wait_all(ag_recv, q)
        wait_all(ag_send, q)

    def final_sources(l):
        q = 2 * l + 1
        return (
            grads_hbm.at[q, pl.ds(0, gc), :],
            grads_hbm.at[q, pl.ds(gc, 8 * (width // 128)), pl.ds(width - 128, 128)],
        )

    def final_own(l):
        targets = (wog_hbm.at[l, g], vec_hbm.at[l, g])
        return [
            pltpu.make_async_copy(source, target, fin_own.at[l, m])
            for m, (source, target) in enumerate(zip(final_sources(l), targets))
        ]

    def final_copies(l, owner, to, k):
        if k < 2:
            sources = final_sources(l)
        else:
            sources = (wog_hbm.at[l, owner], vec_hbm.at[l, owner])
        targets = (wog_hbm.at[l, owner], vec_hbm.at[l, owner])
        return [
            pltpu.make_async_remote_copy(
                sources[m], targets[m], fin_send.at[l, k, m], fin_recv.at[l, k, m], (dp, to), device_id_type=MESH
            )
            for m in range(2)
        ]

    def final_send(l):
        for copy in final_copies(l, g, far, 0) + final_copies(l, g, pair, 1) + final_own(l):
            copy.start()

    def final_relay(l):
        for copy in final_copies(l, g, far, 0):
            copy.wait_recv()
        for copy in final_copies(l, far, pair, 2):
            copy.start()

    def final_wait(l):
        for copy in final_own(l):
            copy.wait()
        for copy in final_copies(l, g, far, 0):
            copy.wait_send()
        for copy in final_copies(l, g, pair, 1) + final_copies(l, far, pair, 2):
            copy.wait()

    def within(value, limit, run):
        @pl.when((value >= 0) & (value < limit))
        def _():
            run(jnp.clip(value, 0, limit - 1))

    def at(now, when, run):
        @pl.when(now == when)
        def _():
            run()

    first = items

    def tick(t, carry):
        u = t - first
        within(t - 3, items, feed)
        within(t - 2, items, mix)
        within(t - 4, items, close)
        within(t, items, attend)
        within(u - 1, items, back_feed)
        within(u, items, back_open)
        within(u - 3, items, back_attend)
        within(u - 1, items, back_norm)
        within(t - 1, items, lambda i: relay_block(i, 0))
        within(u - 2, items, lambda j: relay_block(place(j)[2], 1))

        feed_done = u - seqs
        attend_done = u - seqs - 2

        @pl.when((feed_done >= 0) & (lax.rem(feed_done, seqs) == 0) & (feed_done < items))
        def _():
            l = depth - 1 - feed_done // seqs

            @pl.when(feed_done >= seqs)
            def _():
                gathered_part(jnp.minimum(2 * l + 2, 2 * depth - 2))

            pack_feed(l)
            start_all(scatter_copy, 2 * l)

        @pl.when((attend_done >= 0) & (lax.rem(attend_done, seqs) == 0) & (attend_done < items))
        def _():
            l = depth - 1 - attend_done // seqs
            pack_attend(l)
            start_all(scatter_copy, 2 * l + 1)
            reduce_part(2 * l)

        @pl.when((attend_done >= 2) & (lax.rem(attend_done, seqs) == 2) & (attend_done < items))
        def _():
            reduce_part(2 * (depth - 1 - attend_done // seqs) + 1)

        @pl.when((attend_done >= 3) & (lax.rem(attend_done, seqs) == 3) & (attend_done < items))
        def _():
            l = depth - 1 - attend_done // seqs
            gathered_part(2 * l + 1)
            final_send(l)

        return carry

    lax.fori_loop(0, first + items + 3, tick, 0)

    reduce_part(1)
    for l in range(depth - 1, 0, -1):
        final_relay(l)
    gathered_part(0)
    gathered_part(1)
    final_send(0)
    final_relay(0)
    for l in range(depth):
        final_wait(l)
    for s in range(seqs - 2, seqs):
        gx_copy(s).wait()


def shards(
    ndp,
    ngrp,
    activations,
    cotangent,
    lengths,
    triple_weight,
    triple_bias,
    output_weight,
    output_bias,
    first_gain,
    first_shift,
    widen_weight,
    widen_bias,
    shrink_weight,
    narrow_bias,
    second_gain,
    second_shift,
):
    seqs, tokens, gc = activations.shape
    depth = triple_weight.shape[0]
    fc = widen_weight.shape[-1]
    width = gc * ngrp
    heads = gc // HEAD
    items = depth * seqs
    parts = 2 * depth
    assert ngrp == 4 and seqs == 4 and depth == 2 and fc == width and 2 * tokens == 8 * 128
    part_rows = -(-2 * gc // (16 * ndp)) * 16 * ndp
    chunk = part_rows // ndp
    vec_rows = 8 * (width // 128)
    vmem = pl.BlockSpec(memory_space=pltpu.VMEM)
    hbm = pl.BlockSpec(memory_space=pl.ANY)
    smem = pl.BlockSpec(memory_space=pltpu.SMEM)
    dma = pltpu.SemaphoreType.DMA
    V = pltpu.VMEM
    scratch = [
        V((items, gc + ONES, tokens), BF16),
        V((items, 2 * gc, tokens), BF16),
        V((items, heads, tokens, 128), BF16),
        V((items * heads, tokens, tokens), BF16),
        V((items * heads, 1, tokens), F32),
        V((items, width, tokens), BF16),
        V((items, gc + ONES, tokens), BF16),
        V((items, gc, tokens), BF16),
        V((items, 1, tokens), F32),
        V((items, gc + ONES, tokens), BF16),
        V((items, gc, tokens), BF16),
        V((items, 1, tokens), F32),
        V((depth, 3 * gc, gc), BF16),
        V((depth, gc, heads * 128), BF16),
        V((depth, gc, heads * 128), BF16),
        V((depth, 8, heads * 128), F32),
        V((depth, fc, gc), BF16),
        V((depth, gc, fc), BF16),
        V((depth, gc, width), BF16),
        V((depth, gc, width), BF16),
        V((depth, width, 128), F32),
        V((depth, gc, 128), F32),
        V((128, width), F32),
        V((heads, 2 * HEAD, tokens), BF16),
        V((heads, tokens, 128), BF16),
        V((heads, HEAD + ONES, tokens), BF16),
        V((heads, 2 * HEAD, tokens), BF16),
        V((fc, tokens), BF16),
        V((fc, tokens), BF16),
        V((gc, tokens), BF16),
        V((3 * gc, tokens), BF16),
        V((gc, tokens), F32),
        V((2, gc, tokens), F32),
        V((seqs, gc, tokens), F32),
        V((2, tokens, gc), F32),
        V((gc + ONES, fc), F32),
        V((gc, fc), F32),
        V((gc + ONES, width), F32),
        V((gc + ONES, 3 * gc), F32),
        V((depth, 5, gc, 128), F32),
        V((depth, 8, width), F32),
        V((parts, part_rows, width), BF16),
        V((2, ndp - 1, chunk, width), BF16),
        V((4, items, 8, 128), F32),
        V((4, items, ngrp - 1, 8, 128), F32),
        dma((3 * depth + 1,)),
        dma((2,)),
        dma((2, items)),
        dma((2, items)),
        dma((2, items)),
        dma((2, items)),
        dma((2, items)),
        dma((2, items)),
        dma((4, items)),
        dma((4, items)),
        dma((parts,)),
        dma((parts,)),
        dma((parts,)),
        dma((parts,)),
        dma((parts,)),
        dma((depth, 2)),
        dma((depth, 3, 2)),
        dma((depth, 3, 2)),
    ]
    y, gx, grads, wog, vec = pl.pallas_call(
        functools.partial(body, depth, seqs, ndp, ngrp, tokens, gc, fc, part_rows),
        out_shape=(
            jax.ShapeDtypeStruct((seqs, tokens, gc), BF16),
            jax.ShapeDtypeStruct((seqs, tokens, gc), F32),
            jax.ShapeDtypeStruct((parts, part_rows, width), BF16),
            jax.ShapeDtypeStruct((depth, ngrp, gc, width), BF16),
            jax.ShapeDtypeStruct((depth, ngrp, vec_rows, 128), BF16),
        ),
        in_specs=[smem, hbm, vmem, vmem, vmem, hbm] + [vmem] * 9,
        out_specs=(vmem, hbm, hbm, hbm, hbm),
        scratch_shapes=scratch,
        compiler_params=pltpu.CompilerParams(
            collective_id=0, has_side_effects=True, vmem_limit_bytes=63 << 20
        ),
        name="layers",
    )(
        lengths,
        activations,
        cotangent,
        triple_weight.reshape(depth, gc, 3 * gc),
        triple_bias,
        output_weight,
        output_bias,
        first_gain,
        first_shift,
        widen_weight.reshape(depth, gc, fc),
        widen_bias,
        shrink_weight.reshape(depth, fc, gc),
        narrow_bias,
        second_gain,
        second_shift,
    )
    feed = grads[0::2]
    rest = grads[1::2]
    vec = vec.reshape(depth, ngrp, width // 128, 8, 128).transpose(0, 1, 3, 2, 4)
    vec = vec.reshape(depth, ngrp, 8, width).astype(F32)
    mine = lax.dynamic_index_in_dim(vec, lax.axis_index("grp"), 1, keepdims=False)
    shared = vec[:, :, :, :gc]
    return (
        y,
        gx,
        rest[:, gc : 2 * gc, : 3 * gc].astype(F32)[:, None],
        jnp.stack([mine[:, 2, :gc], mine[:, 2, 2 * gc : 3 * gc]], axis=1),
        wog.reshape(depth, width, width).astype(F32),
        mine[:, 1],
        shared[:, :, 6].reshape(depth, width),
        shared[:, :, 7].reshape(depth, width),
        feed[:, :gc].astype(F32)[:, None],
        mine[:, 0],
        feed[:, gc : 2 * gc].astype(F32).transpose(0, 2, 1)[:, None],
        mine[:, 5, :gc],
        mine[:, 3, :gc],
        mine[:, 4, :gc],
    )


def solution(mesh):
    ndp, ngrp = mesh.shape["dp"], mesh.shape["grp"]
    in_specs = (
        P("dp", None, "grp"),
        P("dp", None, "grp"),
        P("dp"),
        P(None, "grp", None, None),
        P(None, None, "grp"),
        P(),
        P(),
        P(),
        P(),
        P(None, "grp", None, None),
        P(None, "grp"),
        P(None, "grp", None, None),
        P(None, "grp"),
        P(None, "grp"),
        P(None, "grp"),
    )
    out_specs = (
        P("dp", None, "grp"),
        P("dp", None, "grp"),
        P(None, "grp", None, None),
        P(None, None, "grp"),
        P(),
        P(),
        P(),
        P(),
        P(None, "grp", None, None),
        P(None, "grp"),
        P(None, "grp", None, None),
        P(None, "grp"),
        P(None, "grp"),
        P(None, "grp"),
    )
    return jax.shard_map(
        functools.partial(shards, ndp, ngrp),
        mesh=mesh,
        in_specs=in_specs,
        out_specs=out_specs,
        check_vma=False,
    )
```

time: 868 us -> 224 us (0.26); the launches traced: 858 us -> 224 us
  waiting for transfers between devices: 219 us -> 0 us
  Pallas kernels: 0 us -> 200 us
  matrix products: 161 us -> 0 us
  blocking collectives: 128 us -> 0 us
  local copies, waits for them, and re-layouts: 131 us -> 16.5 us
  other arithmetic: 121 us -> 6.6 us
  starting transfers between devices: 81.9 us -> 0 us
  between operations: 16.3 us -> 0.69 us
    pallas_call x0 -> x1, Pallas kernels: none -> 200 us  [shards(): pl.pallas_call(functools.partial(body, depth, seqs, ndp, ngrp, tokens, gc...]
    dot_general x34 -> x0, matrix products: 140 us -> none  [the longest x2 31.7 us: layer_forward(): jnp.dot(group_rows, widen_weight[layer_params, 0], preferred_element_type...]
    psum x2 -> x0, waiting for transfers between devices: 134 us -> none  [the longest x1 134 us: shards(): lax.psum((stacked[0], stacked[1], stacked[6], stacked[7], stacked[8], sta...]
    psum x6 -> x0, blocking collectives: 128 us -> none  [the longest x1 47.3 us: shards(): lax.psum((stacked[2], stacked[3], stacked[4], stacked[5]), ('dp', 'grp'))]
    all_to_all x20 -> x0, waiting for transfers between devices: 84.7 us -> none  [the longest x2 20.8 us: layer_forward(): lax.all_to_all(hidden, 'grp', split_axis=2, concat_axis=0, tiled=True)]
    all_to_all x20 -> x0, starting transfers between devices: 81.4 us -> none  [the longest x2 8.99 us: layer_backward(): lax.all_to_all(hidden_grad.reshape(inputs.shape), 'grp', split_axis=0, co...]
    unnamed x270 -> x16, local copies, waits for them, and re-layouts: 76.2 us -> 11.5 us
    unnamed x11 -> x2, other arithmetic: 62.1 us -> 2.61 us
  transfers between devices with their start and end apart: 22 -> 0, of which waited for: 13 -> 0; matrix products, arithmetic and copies ran while one was open for 25% -> 0% of each run, Pallas kernels for 0% -> 0%
where the time goes in v1:
time: 224 us
  Pallas kernels  200 us (89%)
  local copies, waits for them, and re-layouts  16.5 us (7%)
  other arithmetic  6.6 us (3%)
    pallas_call x1, Pallas kernels, shards(): pl.pallas_call(functools.partial(body, depth, seqs, ndp, ngrp, tokens, gc...  200 us
    unnamed x16, local copies, waits for them, and re-layouts  11.5 us

profile of v1, /device:TPU:0, one launch (start us, length us, event | category | flops | bytes accessed | tf_op | source)
XLA Modules:
  0.0 224.0 jit_solution(5130038763838130982)
XLA Ops:
  0.6 0.0 copy-start.1
  0.7 2.3 %copy.50.x_hbm = bf16[4,512,192]{2,1,0:T(8,128)(2,1)} copy(bf16[4,512,192]{1,2,0:T(8,128)(2,1)} %param.15) | data formatting | bytes 1572864 | tf_op args[0]
  2.9 0.0 copy-done.1
  2.9 0.0 copy-start.2
  2.9 1.3 copy.51.ct
  4.2 0.0 copy-done.2
  4.2 1.2 copy.49
  5.4 200.2 %layers.1 = (bf16[4,512,192]{2,1,0:T(8,128)(2,1)}, f32[4,512,192]{2,1,0:T(8,128)}, bf16[4,384,768]{2,1,0:T(8,128)(2,1)}, bf16[2,4,192,768]{3,2,1,0:T(8,128)(2,1)}, bf16[2,4,48,128]{3,2,1,0:T(8,128)(2,1)}) custom-call(s32[4]{0:T(128)} %lens.1, bf16[4,512,192]{2,1,0:T(8,128)(2,1)} %copy.50.x_hbm, bf16[4,512,192]{2,1,0:T(8,128)(2,1)} %copy.51.ct, ...), custom_call_target="tpu_custom_call" | custom-call | tf_op jit(solution)/shard_map/layers/pallas_call | solution.py:804
  205.6 2.2 copy.52
  207.8 2.8 %copy.53 = f32[4,512,192]{1,2,0:T(8,128)} copy(f32[4,512,192]{2,1,0:T(8,128)} %get-tuple-element.53) | data formatting | bytes 3145728
  210.5 0.0 copy-start
  210.5 1.9 fusion.2
  212.5 0.0 copy-start.3
  212.5 1.0 fusion.1
  213.5 0.0 copy-done.3
  213.5 0.7 convert_bitcast_fusion.1
  214.2 0.8 dynamic-slice_bitcast_fusion
  215.0 0.6 pad_maximum_fusion
  215.6 0.0 copy-done
  215.6 2.7 %bitcast_convert_fusion = f32[2,768,768]{2,1,0:T(8,128)} fusion(bf16[2,4,192,768]{3,2,1,0:T(8,128)(2,1)S(1)} %copy-done), kind=kLoop, calls=%fused_computation | loop fusion | flops 1179648 | bytes 7077888 | tf_op jit(solution)/shard_map/convert_element_type | solution.py:848
  218.3 0.6 copy_bitcast_fusion
  218.9 1.0 slice_reduce_fusion
  219.9 0.7 reshape_squeeze.6
  220.6 0.7 reshape_squeeze.7
  221.2 1.6 convert_bitcast_fusion
  222.8 0.6 copy.67
  223.4 0.6 copy_bitcast_fusion.2
  (2 shorter events, 0.0 us)
Async XLA Ops:
  0.6 2.3 %copy-start.1 = (bf16[4,512,192]{1,2,0:T(8,128)(2,1)S(1)}, bf16[4,512,192]{1,2,0:T(8,128)(2,1)}, u32[]{:S(2)}) copy-start(bf16[4,512,192]{1,2,0:T(8,128)(2,1)} %param.16) | copy-start | bytes 2359300
  2.9 1.3 copy-start.2
  210.5 5.1 %copy-start = (bf16[2,4,192,768]{3,2,1,0:T(8,128)(2,1)S(1)}, bf16[2,4,192,768]{3,2,1,0:T(8,128)(2,1)}, u32[]{:S(2)}) copy-start(bf16[2,4,192,768]{3,2,1,0:T(8,128)(2,1)} %get-tuple-element.23) | copy-start | bytes 7077892
  212.5 1.0 copy-start.3
